TPU v7x, 32 devices: a whole 2x2x4 slice. The times are simulated.
32 devices in a mesh: mem: 4 (over x, core), grid: 8 (over z, y).
Axes of the slice: x: 2, y: 2, z: 4, core: 2. Of those that a mesh axis runs over, the one named last changes fastest.
Arguments:
- obs_ensemble: bfloat16 [256, 32, 256], P('mem', 'grid'), may hold values from -6 to 6
- obs_values: bfloat16 [32, 256], P('grid'), may hold values from -6 to 6
- inverse_error: bfloat16 [32, 256], P('grid'), may hold values from 0.5 to 8
- obs_counts: int32 [32], P('grid'), may hold values from 1 to 256, as said below
- loc_offsets: int32 [32, 4], P('grid'), may hold values from -2 to 2, as said below
- background: bfloat16 [256, 256, 320], P('mem', 'grid'), may hold values from -6 to 6
Outputs:
- analysis: bfloat16 [256, 256, 320], P('mem', 'grid')
Inputs may be any that keep to these rules, and one draw needn't show every extreme that they name: `obs_counts`: counts up to about five times their mean; some block in every draw is full. `loc_offsets`: entry 0 of every list is 0 (the block's own observations); the other entries of a list are distinct nonzero offsets.
All inputs are finite; a program needn't handle non-finite values.
Results may differ from a plain program's by a relative error of at most 0.0063.
Values may be sent and summed in bfloat16 or wider, within the bound.
A program may use at most 128 MiB of HBM per device.

v0:
```python
import functools

import jax
import jax.numpy as jnp
from jax import lax
from jax.experimental import pallas as pl
from jax.experimental.pallas import tpu as pltpu
from jax.sharding import PartitionSpec as P

REACH = 2
NS_STEPS = 6
PIECES = 2
FIRST = 2
EARLY = 6
HUB = 0
MESH = pl.DeviceIdType.MESH
HIGHEST = lax.Precision.HIGHEST
NT = (((1,), (1,)), ((), ()))


def dot(a, b):
    return jnp.dot(a, b, precision=HIGHEST, preferred_element_type=jnp.float32)


def kernel(n, grid_n, loc_ref, counts_ref, obs_ref, values_ref, inverse_ref, bg_ref, result,
           mine, near, own_table, tables, raw, state, upper, lower, sent_w, got_w, group_sem, cross_sem,
           obs_send, obs_pass, obs_recv, tab_send, tab_recv, raw_sem, direct_send, pair_send, pass_send,
           state_recv, w_send, w_recv):
    me = lax.axis_index("mem")
    row = lax.axis_index("grid")
    core = lax.rem(me, 2)
    chip = me // 2
    sibling = me + 1 - 2 * core
    rest = n // 2
    local, blocks, slots = obs_ref.shape
    cols, variables = bg_ref.shape[1:]
    members = n * local
    loc_len = loc_ref.shape[1]
    per = cols // blocks
    width = cols * variables
    chunks = PIECES * blocks
    step = width // chunks
    initial = chunks * FIRST // 8
    early = chunks * EARLY // 8
    around = 2 + 2 * REACH

    def at(mem, shift):
        return {"mem": mem, "grid": lax.rem(row + shift + grid_n, grid_n)}

    def rows_of(mem):
        return pl.ds(pl.multiple_of(mem * local, local), local)

    barrier = pltpu.get_barrier_semaphore()
    for p in range(n):
        if p != HUB:
            @pl.when(me != p)
            def _():
                pl.semaphore_signal(barrier, inc=1, device_id=at(p, 0), device_id_type=MESH)

    def raw_copy(b):
        part = pl.ds(b * per, per)
        return pltpu.make_async_copy(bg_ref.at[:, part], raw.at[:, part], raw_sem.at[b])

    for b in range(blocks):
        raw_copy(b).start()
    mine[...] = jnp.swapaxes(obs_ref[...].astype(jnp.float32), 0, 1).astype(jnp.bfloat16)
    values = values_ref[...].astype(jnp.float32)
    inverse = inverse_ref[...].astype(jnp.float32)
    lane = lax.broadcasted_iota(jnp.int32, (1, slots), 1)
    upmost = lax.broadcasted_iota(jnp.int32, (8, slots), 0) == 0
    for b in range(blocks):
        masked = jnp.where(lane < counts_ref[b], inverse[b : b + 1], 0.0)
        entry = jnp.where(upmost, values[b : b + 1], masked)
        own_table[b] = entry
        tables[blocks + b] = entry
    own_rows = rows_of(me)

    @pl.when(me != HUB)
    def _():
        pl.semaphore_wait(barrier, n - 1)
        pl.semaphore_signal(group_sem, inc=1, device_id=at(HUB, 0), device_id_type=MESH)

    @pl.when(me == HUB)
    def _():
        pl.semaphore_wait(group_sem, n - 1)
        for side in (-1, 1):
            pl.semaphore_signal(barrier, inc=1, device_id=at(HUB, side), device_id_type=MESH)


    def obs_copy(i, q):
        return pltpu.make_async_remote_copy(
            src_ref=mine.at[i], dst_ref=near.at[i - 2 * q + REACH, own_rows],
            send_sem=obs_send.at[i, q + 1], recv_sem=obs_recv.at[i - 2 * q + REACH, me],
            device_id=at(2 * (q % rest) + core, q // rest), device_id_type=MESH)

    def own_obs(i, q):
        u = i - 2 * q + REACH
        return pltpu.make_async_copy(mine.at[i], near.at[u, own_rows], obs_recv.at[u, me])

    def obs_passed(u, k):
        rows = rows_of(2 * k + core)
        return pltpu.make_async_remote_copy(
            src_ref=near.at[u, rows], dst_ref=near.at[u, rows],
            send_sem=obs_pass.at[u, k], recv_sem=obs_recv.at[u, 2 * k + core],
            device_id=at(sibling, 0), device_id_type=MESH)

    def await_obs(u, mem):
        ref = near.at[u, rows_of(mem)]
        pltpu.make_async_copy(ref, ref, obs_recv.at[u, mem]).wait()

    def table_copy(side):
        place = 0 if side == 1 else 2 * blocks
        return pltpu.make_async_remote_copy(
            src_ref=own_table, dst_ref=tables.at[pl.ds(place, blocks)],
            send_sem=tab_send.at[(side + 1) // 2], recv_sem=tab_recv.at[(side + 1) // 2],
            device_id=at(me, side), device_id_type=MESH)

    targets = [(i, q) for i in range(blocks) for q in range(-1, rest + 1) if 0 <= i - 2 * q + REACH < around]
    for i, q in targets:
        if 0 <= q < rest:
            @pl.when(chip != q)
            def _():
                obs_copy(i, q).start()

            @pl.when(chip == q)
            def _():
                own_obs(i, q).start()

    def piece(j):
        return pl.ds(j * step, step)

    def direct(k, j):
        part = state.at[own_rows, piece(j)]
        return pltpu.make_async_remote_copy(
            src_ref=part, dst_ref=part, send_sem=direct_send.at[k, j], recv_sem=state_recv.at[me, j],
            device_id=at(lax.rem(me + 2 * k, n), 0), device_id_type=MESH)

    def paired(j):
        part = state.at[own_rows, piece(j)]
        return pltpu.make_async_remote_copy(
            src_ref=part, dst_ref=part, send_sem=pair_send.at[j], recv_sem=state_recv.at[me, j],
            device_id=at(sibling, 0), device_id_type=MESH)

    def passed(k, j):
        source = lax.rem(me + n - 2 * k, n)
        part = state.at[rows_of(source), piece(j)]
        return pltpu.make_async_remote_copy(
            src_ref=part, dst_ref=part, send_sem=pass_send.at[k, j], recv_sem=state_recv.at[source, j],
            device_id=at(sibling, 0), device_id_type=MESH)

    def await_state(source, j):
        ref = state.at[rows_of(source), piece(j)]
        pltpu.make_async_copy(ref, ref, state_recv.at[source, j]).wait()

    def send_state(j):
        for k in range(1, rest):
            direct(k, j).start()
        paired(j).start()

    for b in range(blocks):
        raw_copy(b).wait()
        state[own_rows, b * per * variables : (b + 1) * per * variables] = (
            raw[:, b * per : (b + 1) * per].reshape(local, per * variables))
        for j in range(b * PIECES, (b + 1) * PIECES):
            if j < initial:
                send_state(j)

    @pl.when(me == HUB)
    def _():
        pl.semaphore_wait(barrier, 2)
        for p in range(n):
            if p != HUB:
                pl.semaphore_signal(cross_sem, inc=1, device_id=at(p, 0), device_id_type=MESH)

    @pl.when(me != HUB)
    def _():
        pl.semaphore_wait(cross_sem, 1)

    for i, q in targets:
        if not 0 <= q < rest:
            obs_copy(i, q).start()
    for side in (-1, 1):
        table_copy(side).start()
    for j in range(initial, early):
        send_state(j)

    for u in range(around):
        for k in range(rest):
            await_obs(u, 2 * k + core)
            obs_passed(u, k).start()
    for side in (-1, 1):
        table_copy(side).wait_recv()
    for u in range(around):
        for k in range(rest):
            await_obs(u, 2 * k + 1 - core)

    gram = jnp.zeros((members, members), jnp.float32)
    rhs = jnp.zeros((8, members), jnp.float32)
    for j in range(loc_len):
        offset = loc_ref[me, j]
        wide = near[core + offset + REACH].astype(jnp.float32)
        table = tables[blocks + me + offset]
        distance = jnp.abs(jnp.full((1, slots), offset, jnp.int32)).astype(jnp.float32)
        weight = table[1:2] * (1.0 / (1.0 + distance))
        mean = jnp.sum(wide, axis=0, keepdims=True) * (1.0 / members)
        scaled = ((wide - mean) * weight).astype(jnp.bfloat16)
        innovation = jnp.broadcast_to((table[0:1] - mean) * weight, (8, slots))
        gram = gram + lax.dot_general(scaled, scaled, NT, preferred_element_type=jnp.float32)
        rhs = rhs + lax.dot_general(innovation, scaled.astype(jnp.float32), NT, precision=HIGHEST,
                                    preferred_element_type=jnp.float32)
    across = lax.broadcasted_iota(jnp.int32, (members, members), 0)
    along = lax.broadcasted_iota(jnp.int32, (members, members), 1)
    identity = (across == along).astype(jnp.float32)
    system = identity + gram / (members - 1)
    square = jnp.sum(jnp.sum(system * system, axis=1, keepdims=True), axis=0, keepdims=True)
    scale = jnp.sqrt(square)
    first = system / scale
    middle = 0.5 * (3.0 * identity - first)
    upper[...] = dot(first, middle)
    lower[...] = middle

    def newton(_, carry):
        mid = 1.5 * identity - 0.5 * dot(lower[...], upper[...])
        upper[...] = dot(upper[...], mid)
        lower[...] = dot(mid, lower[...])
        return carry

    lax.fori_loop(0, NS_STEPS - 2, newton, 0)
    middle = 1.5 * identity - 0.5 * dot(lower[...], upper[...])
    root_inv = dot(middle, lower[...]) / jnp.sqrt(scale)
    shift = dot(dot(rhs, root_inv), root_inv) / (members - 1)
    sent_w[...] = (root_inv + shift[0:1]).astype(jnp.bfloat16)

    def weight_copy(k):
        peer = lax.rem(me + k, n)
        return pltpu.make_async_remote_copy(
            src_ref=sent_w.at[rows_of(peer)], dst_ref=got_w.at[me],
            send_sem=w_send.at[k], recv_sem=w_recv.at[me], device_id=at(peer, 0), device_id_type=MESH)

    for k in range(1, rest):
        await_state(lax.rem(me + n - 2 * k, n), 0)
        passed(k, 0).start()
    for k in range(1, n):
        weight_copy(k).start()
    pltpu.make_async_copy(sent_w.at[own_rows], got_w.at[me], w_recv.at[me]).start()
    for j in range(early, chunks):
        send_state(j)
    for source in range(n):
        pltpu.make_async_copy(got_w.at[source], got_w.at[source], w_recv.at[source]).wait()

    for b in range(blocks):
        weights = got_w[b].astype(jnp.float32)
        folded = weights - jnp.sum(weights, axis=1, keepdims=True) * (1.0 / members) + 1.0 / members
        high = folded.astype(jnp.bfloat16)
        low = (folded - high.astype(jnp.float32)).astype(jnp.bfloat16)
        parts = []
        for j in range(b * PIECES, (b + 1) * PIECES):
            if j + 1 < chunks:
                for k in range(1, rest):
                    await_state(lax.rem(me + n - 2 * k, n), j + 1)
                    passed(k, j + 1).start()
            await_state(sibling, j)
            for k in range(1, rest):
                await_state(lax.rem(sibling + n - 2 * k, n), j)
            piece_state = state[:, j * step : (j + 1) * step]
            total = jnp.dot(high, piece_state, preferred_element_type=jnp.float32)
            total = total + jnp.dot(low, piece_state, preferred_element_type=jnp.float32)
            parts.append(total.astype(jnp.bfloat16))
        result[:, b * per : (b + 1) * per] = jnp.concatenate(parts, axis=1).reshape(local, per, variables)

    for i, q in targets:
        if 0 <= q < rest:
            @pl.when(chip != q)
            def _():
                obs_copy(i, q).wait_send()
        else:
            obs_copy(i, q).wait_send()
    for u in range(around):
        for k in range(rest):
            obs_passed(u, k).wait_send()
    for side in (-1, 1):
        table_copy(side).wait_send()
    for k in range(1, n):
        weight_copy(k).wait_send()
    for j in range(chunks):
        paired(j).wait_send()
        for k in range(1, rest):
            direct(k, j).wait_send()
            passed(k, j).wait_send()


def spread(blocks, held_ref, out_ref, sems):
    per = out_ref.shape[1] // blocks
    parts = [pl.ds(b * per, per) for b in range(blocks)]
    copies = [pltpu.make_async_copy(held_ref.at[:, p], out_ref.at[:, p], sems.at[b]) for b, p in enumerate(parts)]
    for copy in copies:
        copy.start()
    for copy in copies:
        copy.wait()


def on_device(n, grid_n, obs_ensemble, obs_values, inverse_error, obs_counts, loc_offsets, background):
    local, blocks, slots = obs_ensemble.shape
    cols, variables = background.shape[1:]
    members = n * local
    width = cols * variables
    chunks = PIECES * blocks
    rest = n // 2
    around = 2 + 2 * REACH
    assert blocks == n and n % 2 == 0
    dma = pltpu.SemaphoreType.DMA
    smem = pl.BlockSpec(memory_space=pltpu.SMEM)
    vmem = pl.BlockSpec(memory_space=pltpu.VMEM)
    whole = pl.BlockSpec(memory_space=pl.ANY)
    held = pl.pallas_call(
        functools.partial(kernel, n, grid_n),
        out_shape=pltpu.VMEM((local, cols, variables), jnp.bfloat16),
        in_specs=[smem, smem, vmem, vmem, vmem, whole],
        out_specs=vmem,
        scratch_shapes=[
            pltpu.VMEM((blocks, local, slots), jnp.bfloat16),
            pltpu.VMEM((around, members, slots), jnp.bfloat16),
            pltpu.VMEM((blocks, 8, slots), jnp.float32),
            pltpu.VMEM((3 * blocks, 8, slots), jnp.float32),
            pltpu.VMEM((local, cols, variables), jnp.bfloat16),
            pltpu.VMEM((members, width), jnp.bfloat16),
            pltpu.VMEM((members, members), jnp.float32),
            pltpu.VMEM((members, members), jnp.float32),
            pltpu.VMEM((members, members), jnp.bfloat16),
            pltpu.VMEM((n, local, members), jnp.bfloat16),
            pltpu.SemaphoreType.REGULAR,
            pltpu.SemaphoreType.REGULAR,
            dma((blocks, rest + 2)),
            dma((around, rest)),
            dma((around, n)),
            dma((2,)),
            dma((2,)),
            dma((blocks,)),
            dma((rest, chunks)),
            dma((chunks,)),
            dma((rest, chunks)),
            dma((n, chunks)),
            dma((n,)),
            dma((n,)),
        ],
        compiler_params=pltpu.CompilerParams(collective_id=0, has_side_effects=True, vmem_limit_bytes=60 * 2**20),
        name="analysis",
    )(loc_offsets, obs_counts, obs_ensemble, obs_values, inverse_error, background)
    return pl.pallas_call(
        functools.partial(spread, blocks),
        out_shape=jax.ShapeDtypeStruct((local, cols, variables), jnp.bfloat16),
        in_specs=[vmem],
        out_specs=whole,
        scratch_shapes=[dma((blocks,))],
        compiler_params=pltpu.CompilerParams(vmem_limit_bytes=16 * 2**20),
        name="spread",
    )(held)


def solution(mesh):
    placed = (
        P("mem", "grid", None),
        P("grid", None),
        P("grid", None),
        P("grid"),
        P("grid", None),
        P("mem", "grid", None),
    )
    body = functools.partial(on_device, mesh.shape["mem"], mesh.shape["grid"])
    return jax.shard_map(body, mesh=mesh, in_specs=placed, out_specs=P("mem", "grid", None), check_vma=False)
```

profile of v0, /device:TPU:1, one launch (start us, length us, event | category | flops | bytes accessed | tf_op | source)
XLA Modules:
  0.0 42.9 jit_solution(15302189877968403736)
XLA Ops:
  0.0 41.7 %analysis.1.held_ref = bf16[64,32,320]{2,1,0:T(8,128)(2,1)S(1)} custom-call(s32[4,4]{1,0:T(4,128)} %loc_ref.1, s32[4]{0:T(128)} %counts_ref.1, bf16[64,4,256]{2,1,0:T(4,128)(2,1)} %obs_ref.1, bf16[4,256]{1,0:T(4,128)(2,1)} %values_ref.1, bf16[4,256]{1,0:T(4,128)(2,1)} %inverse_ref.1, bf16[64,32,320]{2,1,0:T(8,128)(2,1)} %bg_ref.1), custom_call_target="tpu_custom_call" | custom-call | tf_op jit(solution)/shard_map/analysis/pallas_call | solution.py:315
  41.7 1.2 %spread.1 = bf16[64,32,320]{2,1,0:T(8,128)(2,1)} custom-call(bf16[64,32,320]{2,1,0:T(8,128)(2,1)S(1)} %analysis.1.held_ref), custom_call_target="tpu_custom_call" | custom-call | tf_op jit(solution)/shard_map/spread/pallas_call | solution.py:349
where the time goes:
time: 43.1 us; the launch traced here: 42.9 us
  Pallas kernels  42.9 us (100%)
    pallas_call x1, Pallas kernels, on_device(): pl.pallas_call(functools.partial(kernel, n, grid_n), out_shape=pltpu.VMEM...  41.7 us
    pallas_call x1, Pallas kernels, on_device(): pl.pallas_call(functools.partial(spread, blocks), out_shape=jax.ShapeDtyp...  1.17 us

commit v1 on v0

v1 whole, which is shorter than its diff:
```python
import functools

import jax
import jax.numpy as jnp
from jax import lax
from jax.experimental import pallas as pl
from jax.experimental.pallas import tpu as pltpu
from jax.sharding import PartitionSpec as P

REACH = 2
NS_STEPS = 6
PIECES = 2
AHEAD = 2
HUB = 0
OWN = 4
AROUND = OWN + 2 * REACH
MESH = pl.DeviceIdType.MESH
NT = (((1,), (1,)), ((), ()))


def halves(a):
    high = a.astype(jnp.bfloat16)
    return high, (a - high.astype(jnp.float32)).astype(jnp.bfloat16)


def dot(a, b):
    left = jnp.concatenate([a[0], a[0], a[1]], axis=1)
    right = jnp.concatenate([b[0], b[1], b[0]], axis=0)
    return jnp.dot(left, right, preferred_element_type=jnp.float32)


def kernel(n, grid_n, loc_ref, counts_ref, obs_ref, values_ref, inverse_ref, bg_ref, result,
           obs_in, values_in, inverse_in, mine, near, own_table, tables, raw, state, sent_w, got_w,
           group_sem, cross_sem, in_sem, obs_send, obs_pass, edge_send, obs_recv, tab_send, tab_recv, raw_sem,
           direct_send, pair_send, pass_send, state_recv, w_send, w_recv):
    me = lax.axis_index("mem")
    row = lax.axis_index("grid")
    core = lax.rem(me, 2)
    chip = me // 2
    side = lax.rem(chip, 2)
    pair = chip // 2
    sibling = me + 1 - 2 * core
    far = me + 2 - 4 * side
    rest = n // 2
    pairs = rest // 2
    relay = pairs == 1
    local, blocks, slots = obs_ref.shape
    cols, variables = bg_ref.shape[1:]
    members = n * local
    loc_len = loc_ref.shape[1]
    per = cols // blocks
    width = cols * variables
    chunks = PIECES * blocks
    step = width // chunks

    def at(mem, shift):
        return {"mem": mem, "grid": lax.rem(row + shift + grid_n, grid_n)}

    def rows_of(mem):
        return pl.ds(pl.multiple_of(mem * local, local), local)

    barrier = pltpu.get_barrier_semaphore()
    for p in range(n):
        if p != HUB:
            @pl.when(me != p)
            def _():
                pl.semaphore_signal(barrier, inc=1, device_id=at(p, 0), device_id_type=MESH)

    inputs = [pltpu.make_async_copy(source, target, in_sem.at[k]) for k, (source, target) in enumerate(
        ((obs_ref, obs_in), (values_ref, values_in), (inverse_ref, inverse_in)))]
    for copy in inputs:
        copy.start()

    def raw_copy(b):
        part = pl.ds(b * per, per)
        return pltpu.make_async_copy(bg_ref.at[:, part], raw.at[:, part], raw_sem.at[b])

    for b in range(blocks):
        raw_copy(b).start()
    own_rows = rows_of(me)
    inputs[0].wait()
    mine[...] = jnp.swapaxes(obs_in[...].astype(jnp.float32), 0, 1).astype(jnp.bfloat16)

    @pl.when(me != HUB)
    def _():
        pl.semaphore_wait(barrier, n - 1)
        pl.semaphore_signal(group_sem, inc=1, device_id=at(HUB, 0), device_id_type=MESH)

    @pl.when(me == HUB)
    def _():
        pl.semaphore_wait(group_sem, n - 1)
        for move in (-1, 1):
            pl.semaphore_signal(barrier, inc=1, device_id=at(HUB, move), device_id_type=MESH)

    def chip_of(i, t):
        return 2 * (i // OWN) + t

    def place_of(i):
        return i % OWN + REACH

    def obs_copy(i, t):
        return pltpu.make_async_remote_copy(
            src_ref=mine.at[i], dst_ref=near.at[place_of(i), own_rows],
            send_sem=obs_send.at[i, t], recv_sem=obs_recv.at[place_of(i), me],
            device_id=at(2 * chip_of(i, t) + core, 0), device_id_type=MESH)

    def obs_kept(i):
        return pltpu.make_async_copy(mine.at[i], near.at[place_of(i), own_rows], obs_recv.at[place_of(i), me])

    def obs_shared(i):
        return pltpu.make_async_remote_copy(
            src_ref=mine.at[i], dst_ref=near.at[place_of(i), own_rows],
            send_sem=obs_pass.at[place_of(i), 0], recv_sem=obs_recv.at[place_of(i), me],
            device_id=at(sibling, 0), device_id_type=MESH)

    def obs_passed(u, k):
        source = lax.rem(me + 2 * k, n)
        rows = rows_of(source)
        return pltpu.make_async_remote_copy(
            src_ref=near.at[u, rows], dst_ref=near.at[u, rows],
            send_sem=obs_pass.at[u, k], recv_sem=obs_recv.at[u, source],
            device_id=at(sibling, 0), device_id_type=MESH)

    def await_obs(u, mem):
        ref = near.at[u, rows_of(mem)]
        pltpu.make_async_copy(ref, ref, obs_recv.at[u, mem]).wait()

    def edge_of(i):
        upper = i % OWN >= REACH
        p = i // OWN + (1 if upper else -1)
        u = i % OWN - REACH if upper else i % OWN + OWN + REACH
        return p % pairs, p // pairs, u, 0 if upper else 1

    def edge_copy(i, t, source_ref, member):
        p, shift, u, c = edge_of(i)
        target = 2 * (2 * p + (side if relay else t)) + c
        return target, shift, lambda: pltpu.make_async_remote_copy(
            src_ref=source_ref, dst_ref=near.at[u, rows_of(member)],
            send_sem=edge_send.at[i, t], recv_sem=obs_recv.at[u, member],
            device_id=at(target, shift), device_id_type=MESH)

    def own_edge(i, t):
        return edge_copy(i, t, mine.at[i], me)

    def far_edge(i):
        return edge_copy(i, 1, near.at[place_of(i), rows_of(far)], far)[2]

    def edge_kept(i):
        u = edge_of(i)[2]
        return pltpu.make_async_copy(mine.at[i], near.at[u, own_rows], obs_recv.at[u, me])

    def table_copy(move):
        source, place = (blocks - REACH, 0) if move == 1 else (0, REACH + blocks)
        return pltpu.make_async_remote_copy(
            src_ref=own_table.at[pl.ds(source, REACH)], dst_ref=tables.at[pl.ds(place, REACH)],
            send_sem=tab_send.at[(move + 1) // 2], recv_sem=tab_recv.at[(move + 1) // 2],
            device_id=at(me, move), device_id_type=MESH)

    edge_sides = (0,) if relay else (0, 1)
    for i in range(blocks):
        for t in (0, 1):
            @pl.when(chip != chip_of(i, t))
            def _():
                obs_copy(i, t).start()

            @pl.when(chip == chip_of(i, t))
            def _():
                obs_kept(i).start()
                obs_shared(i).start()
        for t in edge_sides:
            target, shift, copy = own_edge(i, t)
            if shift == 0:
                @pl.when(me != target)
                def _():
                    copy().start()

                @pl.when(me == target)
                def _():
                    edge_kept(i).start()

    def piece(j):
        return pl.ds(j * step, step)

    def direct(k, j):
        part = state.at[own_rows, piece(j)]
        return pltpu.make_async_remote_copy(
            src_ref=part, dst_ref=part, send_sem=direct_send.at[k, j], recv_sem=state_recv.at[me, j],
            device_id=at(lax.rem(me + 2 * k, n), 0), device_id_type=MESH)

    def paired(j):
        part = state.at[own_rows, piece(j)]
        return pltpu.make_async_remote_copy(
            src_ref=part, dst_ref=part, send_sem=pair_send.at[j], recv_sem=state_recv.at[me, j],
            device_id=at(sibling, 0), device_id_type=MESH)

    def passed(k, j):
        source = lax.rem(me + n - 2 * k, n)
        part = state.at[rows_of(source), piece(j)]
        return pltpu.make_async_remote_copy(
            src_ref=part, dst_ref=part, send_sem=pass_send.at[k, j], recv_sem=state_recv.at[source, j],
            device_id=at(sibling, 0), device_id_type=MESH)

    def await_state(source, j):
        ref = state.at[rows_of(source), piece(j)]
        pltpu.make_async_copy(ref, ref, state_recv.at[source, j]).wait()

    def pass_on(j):
        for k in range(1, rest):
            await_state(lax.rem(me + n - 2 * k, n), j)
            passed(k, j).start()

    def flatten(b):
        raw_copy(b).wait()
        state[own_rows, b * per * variables : (b + 1) * per * variables] = (
            raw[:, b * per : (b + 1) * per].reshape(local, per * variables))
        for j in range(b * PIECES, (b + 1) * PIECES):
            for k in range(1, rest):
                direct(k, j).start()
            paired(j).start()

    flatten(0)
    inputs[1].wait()
    inputs[2].wait()
    values = values_in[...].astype(jnp.float32)
    inverse = inverse_in[...].astype(jnp.float32)
    lane = lax.broadcasted_iota(jnp.int32, (1, slots), 1)
    upmost = lax.broadcasted_iota(jnp.int32, (8, slots), 0) == 0
    for b in range(blocks):
        masked = jnp.where(lane < counts_ref[b], inverse[b : b + 1], 0.0)
        entry = jnp.where(upmost, values[b : b + 1], masked)
        own_table[b] = entry
        tables[REACH + b] = entry

    @pl.when(me == HUB)
    def _():
        pl.semaphore_wait(barrier, 2)
        for p in range(n):
            if p != HUB:
                pl.semaphore_signal(cross_sem, inc=1, device_id=at(p, 0), device_id_type=MESH)

    @pl.when(me != HUB)
    def _():
        pl.semaphore_wait(cross_sem, 1)

    for i in range(blocks):
        for t in edge_sides:
            _, shift, copy = own_edge(i, t)
            if shift != 0:
                copy().start()
    for move in (-1, 1):
        table_copy(move).start()
    for b in range(1, blocks):
        flatten(b)

    for u in range(REACH, REACH + OWN):
        for k in range(1, rest):
            await_obs(u, lax.rem(me + 2 * k, n))
            obs_passed(u, k).start()
        if relay:
            far_edge(u - REACH)().start()
    for u in range(REACH, REACH + OWN):
        await_obs(u, me)
        for k in range(rest):
            await_obs(u, 2 * k + 1 - core)

    def products(u):
        wide = near[u].astype(jnp.float32)
        table = tables[OWN * pair + u]
        mean = jnp.sum(wide, axis=0, keepdims=True) * (1.0 / members)
        scaled = ((wide - mean) * table[1:2]).astype(jnp.bfloat16)
        full = (table[0:1] - mean) * table[1:2]
        high = halves(full)
        low = (full - high[0].astype(jnp.float32) - high[1].astype(jnp.float32)).astype(jnp.bfloat16)
        place = lax.broadcasted_iota(jnp.int32, (16, slots), 0)
        lines = jnp.where(place == 0, high[0].astype(jnp.float32), jnp.where(
            place == 1, high[1].astype(jnp.float32), jnp.where(place == 2, low.astype(jnp.float32), 0.0)))
        left = jnp.concatenate([scaled, lines.astype(jnp.bfloat16)], axis=0)
        return lax.dot_general(left, scaled, NT, preferred_element_type=jnp.float32)

    totals = [jnp.zeros((members + 16, members), jnp.float32) for _ in range(2)]

    def add(u):
        found = products(u)
        for t in range(2):
            distance = u - REACH - 2 * core - t
            away = jnp.abs(distance)
            share = jnp.where(away == 0, 1.0, jnp.where(away == 1, 1.0 / 4.0, 1.0 / 9.0))
            taken = 0.0
            for j in range(loc_len):
                taken = taken + jnp.where(loc_ref[OWN * pair + 2 * core + t, j] == distance, share, 0.0)
            totals[t] = totals[t] + taken * found

    for u in range(REACH, REACH + OWN):
        add(u)
    for move in (-1, 1):
        table_copy(move).wait_recv()
    for e in range(REACH):
        u = e + (OWN + REACH) * core
        for source in range(n):
            await_obs(u, source)
        add(u)

    for j in range(AHEAD):
        pass_on(j)
    across = lax.broadcasted_iota(jnp.int32, (members, members), 0)
    along = lax.broadcasted_iota(jnp.int32, (members, members), 1)
    identity = (across == along).astype(jnp.float32)
    scales, uppers, lowers = [], [], []
    for t in range(2):
        system = identity + totals[t][:members] / (members - 1)
        square = jnp.sum(jnp.sum(system * system, axis=1, keepdims=True), axis=0, keepdims=True)
        scale = jnp.sqrt(square)
        first = system / scale
        middle = halves(1.5 * identity - 0.5 * first)
        scales.append(scale)
        uppers.append(halves(dot(halves(first), middle)))
        lowers.append(middle)
    for s in range(1, NS_STEPS):
        middles = [halves(1.5 * identity - 0.5 * dot(lowers[t], uppers[t])) for t in range(2)]
        if s < NS_STEPS - 1:
            uppers = [halves(dot(uppers[t], middles[t])) for t in range(2)]
            lowers = [halves(dot(middles[t], lowers[t])) for t in range(2)]
        else:
            roots = [dot(middles[t], lowers[t]) / jnp.sqrt(scales[t]) for t in range(2)]
    for t in range(2):
        root = halves(roots[t])
        lines = totals[t][members:]
        rhs = lines[0:1] + lines[1:2] + lines[2:3]
        rhs = jnp.broadcast_to(rhs, (16, members))
        shift = dot(halves(dot(halves(rhs), root)), root) / (members - 1)
        sent_w[t] = (roots[t] + shift[0:1]).astype(jnp.bfloat16)

    slot = OWN * pair + 2 * core

    def weight_copy(k):
        p, c = lax.rem(pair + k // 2, pairs), core if k % 2 == 0 else 1 - core
        peer = 4 * p + 2 * side + c
        return pltpu.make_async_remote_copy(
            src_ref=sent_w.at[:, rows_of(peer)], dst_ref=got_w.at[pl.ds(slot, 2)],
            send_sem=w_send.at[k], recv_sem=w_recv.at[me // 4, core], device_id=at(peer, 0), device_id_type=MESH)

    for k in range(1, 2 * pairs):
        weight_copy(k).start()
    pltpu.make_async_copy(sent_w.at[:, own_rows], got_w.at[pl.ds(slot, 2)], w_recv.at[pair, core]).start()
    for p in range(pairs):
        for c in range(2):
            part = got_w.at[pl.ds(OWN * p + 2 * c, 2)]
            pltpu.make_async_copy(part, part, w_recv.at[p, c]).wait()

    for b in range(blocks):
        weights = got_w[b].astype(jnp.float32)
        folded = weights - jnp.sum(weights, axis=1, keepdims=True) * (1.0 / members) + 1.0 / members
        both = jnp.concatenate(halves(folded), axis=0)
        parts = []
        for j in range(b * PIECES, (b + 1) * PIECES):
            if j + 1 < chunks and j + 1 >= AHEAD:
                pass_on(j + 1)
            await_state(sibling, j)
            for k in range(1, rest):
                await_state(lax.rem(sibling + n - 2 * k, n), j)
            total = jnp.dot(both, state[:, j * step : (j + 1) * step], preferred_element_type=jnp.float32)
            parts.append((total[:local] + total[local:]).astype(jnp.bfloat16))
        result[:, b * per : (b + 1) * per] = jnp.concatenate(parts, axis=1).reshape(local, per, variables)

    for i in range(blocks):
        for t in (0, 1):
            @pl.when(chip != chip_of(i, t))
            def _():
                obs_copy(i, t).wait_send()

            @pl.when(chip == chip_of(i, t))
            def _():
                obs_shared(i).wait_send()
        for t in edge_sides:
            target, shift, copy = own_edge(i, t)
            if shift == 0:
                @pl.when(me != target)
                def _():
                    copy().wait_send()
            else:
                copy().wait_send()
        if relay:
            far_edge(i)().wait_send()
    for u in range(REACH, REACH + OWN):
        for k in range(1, rest):
            obs_passed(u, k).wait_send()
    for move in (-1, 1):
        table_copy(move).wait_send()
    for k in range(1, 2 * pairs):
        weight_copy(k).wait_send()
    for j in range(chunks):
        paired(j).wait_send()
        for k in range(1, rest):
            direct(k, j).wait_send()
            passed(k, j).wait_send()


def spread(blocks, held_ref, out_ref, sems):
    per = out_ref.shape[1] // blocks
    parts = [pl.ds(b * per, per) for b in range(blocks)]
    copies = [pltpu.make_async_copy(held_ref.at[:, p], out_ref.at[:, p], sems.at[b]) for b, p in enumerate(parts)]
    for copy in copies:
        copy.start()
    for copy in copies:
        copy.wait()


def on_device(n, grid_n, obs_ensemble, obs_values, inverse_error, obs_counts, loc_offsets, background):
    local, blocks, slots = obs_ensemble.shape
    cols, variables = background.shape[1:]
    members = n * local
    width = cols * variables
    chunks = PIECES * blocks
    rest = n // 2
    assert blocks == n and n % 4 == 0
    dma = pltpu.SemaphoreType.DMA
    smem = pl.BlockSpec(memory_space=pltpu.SMEM)
    vmem = pl.BlockSpec(memory_space=pltpu.VMEM)
    whole = pl.BlockSpec(memory_space=pl.ANY)
    held = pl.pallas_call(
        functools.partial(kernel, n, grid_n),
        out_shape=pltpu.VMEM((local, cols, variables), jnp.bfloat16),
        in_specs=[smem, smem, whole, whole, whole, whole],
        out_specs=vmem,
        scratch_shapes=[
            pltpu.VMEM((local, blocks, slots), jnp.bfloat16),
            pltpu.VMEM((blocks, slots), jnp.bfloat16),
            pltpu.VMEM((blocks, slots), jnp.bfloat16),
            pltpu.VMEM((blocks, local, slots), jnp.bfloat16),
            pltpu.VMEM((AROUND, members, slots), jnp.bfloat16),
            pltpu.VMEM((blocks, 8, slots), jnp.float32),
            pltpu.VMEM((blocks + 2 * REACH, 8, slots), jnp.float32),
            pltpu.VMEM((local, cols, variables), jnp.bfloat16),
            pltpu.VMEM((members, width), jnp.bfloat16),
            pltpu.VMEM((2, members, members), jnp.bfloat16),
            pltpu.VMEM((n, local, members), jnp.bfloat16),
            pltpu.SemaphoreType.REGULAR,
            pltpu.SemaphoreType.REGULAR,
            dma((3,)),
            dma((blocks, 2)),
            dma((AROUND, rest)),
            dma((blocks, 2)),
            dma((AROUND, n)),
            dma((2,)),
            dma((2,)),
            dma((blocks,)),
            dma((rest, chunks)),
            dma((chunks,)),
            dma((rest, chunks)),
            dma((n, chunks)),
            dma((n,)),
            dma((rest // 2, 2)),
        ],
        compiler_params=pltpu.CompilerParams(collective_id=0, has_side_effects=True, vmem_limit_bytes=60 * 2**20),
        name="analysis",
    )(loc_offsets, obs_counts, obs_ensemble, obs_values, inverse_error, background)
    return pl.pallas_call(
        functools.partial(spread, blocks),
        out_shape=jax.ShapeDtypeStruct((local, cols, variables), jnp.bfloat16),
        in_specs=[vmem],
        out_specs=whole,
        scratch_shapes=[dma((blocks,))],
        compiler_params=pltpu.CompilerParams(vmem_limit_bytes=16 * 2**20),
        name="spread",
    )(held)


def solution(mesh):
    placed = (
        P("mem", "grid", None),
        P("grid", None),
        P("grid", None),
        P("grid"),
        P("grid", None),
        P("mem", "grid", None),
    )
    body = functools.partial(on_device, mesh.shape["mem"], mesh.shape["grid"])
    return jax.shard_map(body, mesh=mesh, in_specs=placed, out_specs=P("mem", "grid", None), check_vma=False)
```

time: 43.1 us -> 40.5 us (0.940)
  Pallas kernels: 42.9 us -> 40.3 us
    pallas_call x1, Pallas kernels: 41.7 us -> 39.2 us  [on_device(): pl.pallas_call(functools.partial(kernel, n, grid_n), out_shape=pltpu.VMEM...]
where the time goes in v1:
time: 40.5 us; the launch traced here: 40.3 us
  Pallas kernels  40.3 us (100%)
    pallas_call x1, Pallas kernels, on_device(): pl.pallas_call(functools.partial(kernel, n, grid_n), out_shape=pltpu.VMEM...  39.2 us
    pallas_call x1, Pallas kernels, on_device(): pl.pallas_call(functools.partial(spread, blocks), out_shape=jax.ShapeDtyp...  1.17 us

profile of v1, /device:TPU:1, one launch (start us, length us, event | category | flops | bytes accessed | tf_op | source)
XLA Modules:
  0.0 40.3 jit_solution(8456182192360534775)
XLA Ops:
  0.0 39.2 %analysis.1.held_ref = bf16[64,32,320]{2,1,0:T(8,128)(2,1)S(1)} custom-call(s32[4,4]{1,0:T(4,128)} %loc_ref.1, s32[4]{0:T(128)} %counts_ref.1, bf16[64,4,256]{2,1,0:T(4,128)(2,1)} %obs_ref.1, bf16[4,256]{1,0:T(4,128)(2,1)} %values_ref.1, bf16[4,256]{1,0:T(4,128)(2,1)} %inverse_ref.1, bf16[64,32,320]{2,1,0:T(8,128)(2,1)} %bg_ref.1), custom_call_target="tpu_custom_call" | custom-call | tf_op jit(solution)/shard_map/analysis/pallas_call | solution.py:420
  39.2 1.2 %spread.1 = bf16[64,32,320]{2,1,0:T(8,128)(2,1)} custom-call(bf16[64,32,320]{2,1,0:T(8,128)(2,1)S(1)} %analysis.1.held_ref), custom_call_target="tpu_custom_call" | custom-call | tf_op jit(solution)/shard_map/spread/pallas_call | solution.py:457

commit v2 on v1

--- a/solution.py
+++ b/solution.py
@@ -9,7 +9,6 @@
 
 REACH = 2
 NS_STEPS = 6
-PIECES = 2
 AHEAD = 2
 HUB = 0
 OWN = 4
@@ -29,9 +28,18 @@
     return jnp.dot(left, right, preferred_element_type=jnp.float32)
 
 
-def kernel(n, grid_n, loc_ref, counts_ref, obs_ref, values_ref, inverse_ref, bg_ref, result,
-           obs_in, values_in, inverse_in, mine, near, own_table, tables, raw, state, sent_w, got_w,
-           group_sem, cross_sem, in_sem, obs_send, obs_pass, edge_send, obs_recv, tab_send, tab_recv, raw_sem,
+def cut(blocks, per):
+    cuts = []
+    for b in range(blocks):
+        sizes = [per // 2, per // 2] if b + 1 < blocks else [per // 2, per // 4, per // 4]
+        for size in sizes:
+            cuts.append((cuts[-1][0] + cuts[-1][1] if cuts else 0, size))
+    return cuts
+
+
+def kernel(n, grid_n, loc_in, counts_in, obs_ref, values_ref, inverse_ref, bg_ref, result,
+           loc_ref, counts_ref, obs_in, obs_far, values_in, inverse_in, mine, near, own_table, tables, raw, state, sent_w, got_w,
+           group_sem, cross_sem, in_sem, far_send, far_recv, obs_send, obs_pass, edge_send, obs_recv, tab_send, tab_recv, raw_sem,
            direct_send, pair_send, pass_send, state_recv, w_send, w_recv):
     me = lax.axis_index("mem")
     row = lax.axis_index("grid")
@@ -47,11 +55,8 @@
     local, blocks, slots = obs_ref.shape
     cols, variables = bg_ref.shape[1:]
     members = n * local
-    loc_len = loc_ref.shape[1]
+    loc_len = loc_in.shape[1]
     per = cols // blocks
-    width = cols * variables
-    chunks = PIECES * blocks
-    step = width // chunks
 
     def at(mem, shift):
         return {"mem": mem, "grid": lax.rem(row + shift + grid_n, grid_n)}
@@ -67,19 +72,20 @@
                 pl.semaphore_signal(barrier, inc=1, device_id=at(p, 0), device_id_type=MESH)
 
     inputs = [pltpu.make_async_copy(source, target, in_sem.at[k]) for k, (source, target) in enumerate(
-        ((obs_ref, obs_in), (values_ref, values_in), (inverse_ref, inverse_in)))]
-    for copy in inputs:
-        copy.start()
-
+        ((obs_ref, obs_in), (values_ref, values_in), (inverse_ref, inverse_in), (loc_in, loc_ref), (counts_in, counts_ref)))]
     def raw_copy(b):
         part = pl.ds(b * per, per)
         return pltpu.make_async_copy(bg_ref.at[:, part], raw.at[:, part], raw_sem.at[b])
 
-    for b in range(blocks):
+    raw_copy(0).start()
+    for copy in inputs:
+        copy.start()
+    for b in range(1, blocks):
         raw_copy(b).start()
     own_rows = rows_of(me)
-    inputs[0].wait()
-    mine[...] = jnp.swapaxes(obs_in[...].astype(jnp.float32), 0, 1).astype(jnp.bfloat16)
+
+    def reordered(ref):
+        return jnp.swapaxes(ref[...].astype(jnp.float32), 0, 1).astype(jnp.bfloat16)
 
     @pl.when(me != HUB)
     def _():
@@ -91,6 +97,12 @@
         pl.semaphore_wait(group_sem, n - 1)
         for move in (-1, 1):
             pl.semaphore_signal(barrier, inc=1, device_id=at(HUB, move), device_id_type=MESH)
+
+    far_copy = pltpu.make_async_remote_copy(
+        src_ref=obs_ref, dst_ref=obs_far, send_sem=far_send, recv_sem=far_recv,
+        device_id=at(far, 0), device_id_type=MESH)
+    if relay:
+        far_copy.start()
 
     def chip_of(i, t):
         return 2 * (i // OWN) + t
@@ -157,29 +169,40 @@
             device_id=at(me, move), device_id_type=MESH)
 
     edge_sides = (0,) if relay else (0, 1)
-    for i in range(blocks):
-        for t in (0, 1):
-            @pl.when(chip != chip_of(i, t))
-            def _():
-                obs_copy(i, t).start()
-
-            @pl.when(chip == chip_of(i, t))
-            def _():
+
+    def send_obs():
+        inputs[0].wait()
+        mine[...] = reordered(obs_in)
+        for i in range(blocks):
+            if relay:
                 obs_kept(i).start()
                 obs_shared(i).start()
-        for t in edge_sides:
-            target, shift, copy = own_edge(i, t)
-            if shift == 0:
-                @pl.when(me != target)
+                continue
+            for t in (0, 1):
+                @pl.when(chip != chip_of(i, t))
                 def _():
-                    copy().start()
-
-                @pl.when(me == target)
+                    obs_copy(i, t).start()
+
+                @pl.when(chip == chip_of(i, t))
                 def _():
-                    edge_kept(i).start()
+                    obs_kept(i).start()
+                    obs_shared(i).start()
+                target, shift, copy = own_edge(i, t)
+                if shift == 0:
+                    @pl.when(me != target)
+                    def _():
+                        copy().start()
+
+                    @pl.when(me == target)
+                    def _():
+                        edge_kept(i).start()
+
+    cuts = cut(blocks, per)
+    chunks = len(cuts)
+    pieces_of = [[j for j, (first, _) in enumerate(cuts) if first // per == b] for b in range(blocks)]
 
     def piece(j):
-        return pl.ds(j * step, step)
+        return pl.ds(cuts[j][0] * variables, cuts[j][1] * variables)
 
     def direct(k, j):
         part = state.at[own_rows, piece(j)]
@@ -213,14 +236,15 @@
         raw_copy(b).wait()
         state[own_rows, b * per * variables : (b + 1) * per * variables] = (
             raw[:, b * per : (b + 1) * per].reshape(local, per * variables))
-        for j in range(b * PIECES, (b + 1) * PIECES):
+        for j in pieces_of[b]:
             for k in range(1, rest):
                 direct(k, j).start()
             paired(j).start()
 
     flatten(0)
-    inputs[1].wait()
-    inputs[2].wait()
+    send_obs()
+    for copy in inputs[1:]:
+        copy.wait()
     values = values_in[...].astype(jnp.float32)
     inverse = inverse_in[...].astype(jnp.float32)
     lane = lax.broadcasted_iota(jnp.int32, (1, slots), 1)
@@ -252,9 +276,13 @@
     for b in range(1, blocks):
         flatten(b)
 
+    if relay:
+        far_copy.wait_recv()
+        near[REACH : REACH + OWN, rows_of(far)] = reordered(obs_far)
     for u in range(REACH, REACH + OWN):
         for k in range(1, rest):
-            await_obs(u, lax.rem(me + 2 * k, n))
+            if not relay:
+                await_obs(u, lax.rem(me + 2 * k, n))
             obs_passed(u, k).start()
         if relay:
             far_edge(u - REACH)().start()
@@ -347,52 +375,60 @@
             part = got_w.at[pl.ds(OWN * p + 2 * c, 2)]
             pltpu.make_async_copy(part, part, w_recv.at[p, c]).wait()
 
+    def settle():
+        if relay:
+            far_copy.wait_send()
+        for i in range(blocks):
+            for t in (0, 1):
+                if relay:
+                    continue
+                @pl.when(chip != chip_of(i, t))
+                def _():
+                    obs_copy(i, t).wait_send()
+
+                @pl.when(chip == chip_of(i, t))
+                def _():
+                    obs_shared(i).wait_send()
+            if relay:
+                obs_shared(i).wait_send()
+                far_edge(i)().wait_send()
+            for t in edge_sides:
+                target, shift, copy = own_edge(i, t)
+                if shift == 0:
+                    @pl.when(me != target)
+                    def _():
+                        copy().wait_send()
+                else:
+                    copy().wait_send()
+        for u in range(REACH, REACH + OWN):
+            for k in range(1, rest):
+                obs_passed(u, k).wait_send()
+        for move in (-1, 1):
+            table_copy(move).wait_send()
+        for k in range(1, 2 * pairs):
+            weight_copy(k).wait_send()
+        for j in range(chunks):
+            paired(j).wait_send()
+            for k in range(1, rest):
+                direct(k, j).wait_send()
+                passed(k, j).wait_send()
+
     for b in range(blocks):
         weights = got_w[b].astype(jnp.float32)
         folded = weights - jnp.sum(weights, axis=1, keepdims=True) * (1.0 / members) + 1.0 / members
         both = jnp.concatenate(halves(folded), axis=0)
         parts = []
-        for j in range(b * PIECES, (b + 1) * PIECES):
-            if j + 1 < chunks and j + 1 >= AHEAD:
+        for j in pieces_of[b]:
+            if AHEAD <= j + 1 < chunks:
                 pass_on(j + 1)
+            if j == chunks - 1:
+                settle()
             await_state(sibling, j)
             for k in range(1, rest):
                 await_state(lax.rem(sibling + n - 2 * k, n), j)
-            total = jnp.dot(both, state[:, j * step : (j + 1) * step], preferred_element_type=jnp.float32)
+            total = jnp.dot(both, state[:, piece(j)], preferred_element_type=jnp.float32)
             parts.append((total[:local] + total[local:]).astype(jnp.bfloat16))
         result[:, b * per : (b + 1) * per] = jnp.concatenate(parts, axis=1).reshape(local, per, variables)
-
-    for i in range(blocks):
-        for t in (0, 1):
-            @pl.when(chip != chip_of(i, t))
-            def _():
-                obs_copy(i, t).wait_send()
-
-            @pl.when(chip == chip_of(i, t))
-            def _():
-                obs_shared(i).wait_send()
-        for t in edge_sides:
-            target, shift, copy = own_edge(i, t)
-            if shift == 0:
-                @pl.when(me != target)
-                def _():
-                    copy().wait_send()
-            else:
-                copy().wait_send()
-        if relay:
-            far_edge(i)().wait_send()
-    for u in range(REACH, REACH + OWN):
-        for k in range(1, rest):
-            obs_passed(u, k).wait_send()
-    for move in (-1, 1):
-        table_copy(move).wait_send()
-    for k in range(1, 2 * pairs):
-        weight_copy(k).wait_send()
-    for j in range(chunks):
-        paired(j).wait_send()
-        for k in range(1, rest):
-            direct(k, j).wait_send()
-            passed(k, j).wait_send()
 
 
 def spread(blocks, held_ref, out_ref, sems):
@@ -410,19 +446,21 @@
     cols, variables = background.shape[1:]
     members = n * local
     width = cols * variables
-    chunks = PIECES * blocks
+    chunks = len(cut(blocks, cols // blocks))
     rest = n // 2
     assert blocks == n and n % 4 == 0
     dma = pltpu.SemaphoreType.DMA
-    smem = pl.BlockSpec(memory_space=pltpu.SMEM)
     vmem = pl.BlockSpec(memory_space=pltpu.VMEM)
     whole = pl.BlockSpec(memory_space=pl.ANY)
     held = pl.pallas_call(
         functools.partial(kernel, n, grid_n),
         out_shape=pltpu.VMEM((local, cols, variables), jnp.bfloat16),
-        in_specs=[smem, smem, whole, whole, whole, whole],
+        in_specs=[whole] * 6,
         out_specs=vmem,
         scratch_shapes=[
+            pltpu.SMEM(loc_offsets.shape, jnp.int32),
+            pltpu.SMEM(obs_counts.shape, jnp.int32),
+            pltpu.VMEM((local, blocks, slots), jnp.bfloat16),
             pltpu.VMEM((local, blocks, slots), jnp.bfloat16),
             pltpu.VMEM((blocks, slots), jnp.bfloat16),
             pltpu.VMEM((blocks, slots), jnp.bfloat16),
@@ -436,7 +474,9 @@
             pltpu.VMEM((n, local, members), jnp.bfloat16),
             pltpu.SemaphoreType.REGULAR,
             pltpu.SemaphoreType.REGULAR,
-            dma((3,)),
+            dma((5,)),
+            dma(()),
+            dma(()),
             dma((blocks, 2)),
             dma((AROUND, rest)),
             dma((blocks, 2)),

time: 40.5 us -> 39.5 us (0.975)
  Pallas kernels: 40.3 us -> 39.2 us
    pallas_call x1, Pallas kernels: 39.2 us -> 38.1 us  [on_device(): pl.pallas_call(functools.partial(kernel, n, grid_n), out_shape=pltpu.VMEM...]
where the time goes in v2:
time: 39.5 us; the launch traced here: 39.2 us
  Pallas kernels  39.2 us (99%)
    pallas_call x1, Pallas kernels, on_device(): pl.pallas_call(functools.partial(kernel, n, grid_n), out_shape=pltpu.VMEM...  38.1 us
    pallas_call x1, Pallas kernels, on_device(): pl.pallas_call(functools.partial(spread, blocks), out_shape=jax.ShapeDtyp...  1.17 us

profile of v2, /device:TPU:1, one launch (start us, length us, event | category | flops | bytes accessed | tf_op | source)
XLA Modules:
  0.0 39.2 jit_solution(6897249545861921215)
XLA Ops:
  0.0 38.1 %analysis.1.held_ref = bf16[64,32,320]{2,1,0:T(8,128)(2,1)S(1)} custom-call(s32[4,4]{1,0:T(4,128)} %loc_in.1, s32[4]{0:T(128)} %counts_in.1, bf16[64,4,256]{2,1,0:T(4,128)(2,1)} %obs_ref.1, bf16[4,256]{1,0:T(4,128)(2,1)} %values_ref.1, bf16[4,256]{1,0:T(4,128)(2,1)} %inverse_ref.1, bf16[64,32,320]{2,1,0:T(8,128)(2,1)} %bg_ref.1), custom_call_target="tpu_custom_call" | custom-call | tf_op jit(solution)/shard_map/analysis/pallas_call | solution.py:455
  38.1 1.2 %spread.1 = bf16[64,32,320]{2,1,0:T(8,128)(2,1)} custom-call(bf16[64,32,320]{2,1,0:T(8,128)(2,1)S(1)} %analysis.1.held_ref), custom_call_target="tpu_custom_call" | custom-call | tf_op jit(solution)/shard_map/spread/pallas_call | solution.py:497
